TPU v7x, 32 devices: a whole 2x2x4 slice. The times are simulated.
32 devices in a mesh: dp: 4 (over y, x), context: 8 (over z, core).
Axes of the slice: x: 2, y: 2, z: 4, core: 2. Of those that a mesh axis runs over, the one named last changes fastest.
Arguments:
- projected: bfloat16 [4096, 6144], P(('dp', 'context')), may hold values from -6 to 6
- short_taps: float32 [3, 6144], replicated, may hold values from -4 to 4
- long_filter: float32 [2048, 1024], P('context'), may hold values from -1.5 to 1.5
- skip_gain: float32 [2048], P('context'), may hold values from -4 to 4
- out_proj: bfloat16 [2048, 2048], P('dp'), may hold values from -0.125 to 0.125
- cotangent: bfloat16 [4096, 2048], P(('dp', 'context')), may hold values from -25 to 25
Outputs:
- grad_inputs: bfloat16 [4096, 6144], P(('dp', 'context'))
- grad_taps: float32 [3, 6144], replicated
- grad_filter: float32 [2048, 1024], P('context', 'dp')
- grad_skip: float32 [2048], P('context')
- grad_proj: float32 [2048, 2048], P(('dp', 'context'))
All inputs are finite; a program needn't handle non-finite values.
Results may differ from a plain program's by a relative error of at most 0.012.
Values may be sent and summed in bfloat16 or wider, within the bound.
No kernel may reach another device: no remote copies, remote signals or barrier semaphores. Data moves between devices by JAX's collectives and lax.ppermute only.
A program may use at most 128 MiB of HBM per device.

v0:
```python
import math
import jax
import jax.numpy as jnp
from jax import lax
from jax.sharding import PartitionSpec as P

PRECISE = lax.Precision.HIGH


def passed_along(value, axis, steps):
    count = lax.axis_size(axis)
    initial, last = (max(0, -steps), min(count, count - steps))
    return lax.ppermute(value, axis, [(source, source + steps) for source in range(initial, last)])


def angle_table(first_count, second_count, period):
    first_idx = lax.broadcasted_iota(jnp.int32, (first_count, second_count), 0)
    second_idx = lax.broadcasted_iota(jnp.int32, (first_count, second_count), 1)
    phases = first_idx * second_idx % period
    angles = phases.astype(jnp.float32) * (-2.0 * math.pi / period)
    return (jnp.cos(angles), jnp.sin(angles))


def make_tables(seq_len):
    radix_size = min(128, seq_len)
    blocks = 2 * seq_len // radix_size
    half_blocks = blocks // 2
    outer_re, outer_im = angle_table(blocks, blocks, blocks)
    twist = angle_table(blocks, radix_size, blocks * radix_size)
    inner_re, inner_im = angle_table(radix_size, radix_size, radix_size)
    first_table = jnp.concatenate([outer_re[:, :half_blocks], outer_im[:, :half_blocks]], 0)
    inner_fwd = jnp.concatenate(
        [jnp.concatenate([inner_re, inner_im], 1), jnp.concatenate([-inner_im, inner_re], 1)], 0
    )
    inner_back = jnp.concatenate(
        [jnp.concatenate([inner_re, -inner_im], 1), jnp.concatenate([inner_im, inner_re], 1)], 0
    )
    last_table = jnp.concatenate([outer_re[:half_blocks, :], outer_im[:half_blocks, :]], 1)
    return (first_table, twist, inner_fwd, inner_back, last_table)


def forward_spectrum(signal, tables):
    first_table, (twist_re, twist_im), inner_fwd, inner_back, last_table = tables
    blocks = twist_re.shape[0]
    radix_size = twist_re.shape[1]
    shaped = signal.reshape(signal.shape[0], blocks // 2, radix_size)
    first = jnp.einsum("kn,cnm->ckm", first_table, shaped, precision=PRECISE)
    first_re = first[:, :blocks]
    first_im = first[:, blocks:]
    turned = jnp.concatenate(
        [first_re * twist_re - first_im * twist_im, first_re * twist_im + first_im * twist_re], 2
    )
    return jnp.einsum("ckn,nm->ckm", turned, inner_fwd, precision=PRECISE)


def spectral_product(left, right, conjugate_left):
    width = left.shape[2] // 2
    left_re, left_im = (left[:, :, :width], left[:, :, width:])
    right_re, right_im = (right[:, :, :width], right[:, :, width:])
    if conjugate_left:
        return jnp.concatenate(
            [left_re * right_re + left_im * right_im, left_re * right_im - left_im * right_re], 2
        )
    return jnp.concatenate(
        [left_re * right_re - left_im * right_im, left_re * right_im + left_im * right_re], 2
    )


def inverse_real(spectrum, tables):
    first_table, (twist_re, twist_im), inner_fwd, inner_back, last_table = tables
    blocks = twist_re.shape[0]
    radix_size = twist_re.shape[1]
    undo = jnp.einsum("ckn,nm->ckm", spectrum, inner_back, precision=PRECISE)
    undo_re = undo[:, :, :radix_size]
    undo_im = undo[:, :, radix_size:]
    back = jnp.concatenate(
        [undo_re * twist_re + undo_im * twist_im, undo_im * twist_re - undo_re * twist_im], 1
    )
    result = jnp.einsum("nk,ckm->cnm", last_table, back, precision=PRECISE)
    return result.reshape(spectrum.shape[0], blocks // 2 * radix_size) / (blocks * radix_size)


def body(projected, short_taps, long_filter, skip_gain, out_proj, cotangent):
    tok_rows = projected.shape[0]
    chan_all = projected.shape[1] // 3
    prev_rows = passed_along(projected[tok_rows - 2 :], "context", 1)
    extended = jnp.concatenate([prev_rows, projected], 0).astype(jnp.float32)
    current = extended[2:]
    once_back = extended[1 : tok_rows + 1]
    twice_back = extended[:tok_rows]
    mixed = short_taps[0] * current + short_taps[1] * once_back + short_taps[2] * twice_back
    query = mixed[:, :chan_all].astype(jnp.bfloat16)
    keyed = mixed[:, chan_all : 2 * chan_all].astype(jnp.bfloat16)
    valued = mixed[:, 2 * chan_all :].astype(jnp.bfloat16)
    product = (keyed.astype(jnp.float32) * valued.astype(jnp.float32)).astype(jnp.bfloat16)
    product_chan = lax.all_to_all(product.T, "context", split_axis=0, concat_axis=1, tiled=True)
    seq_len = product_chan.shape[1]
    tables = make_tables(seq_len)
    prod_f = product_chan.astype(jnp.float32)
    filter_spec = forward_spectrum(long_filter, tables)
    prod_spec = forward_spectrum(prod_f, tables)
    long_chan = (
        inverse_real(spectral_product(filter_spec, prod_spec, False), tables)
        + skip_gain[:, None] * prod_f
    )
    long_tok = lax.all_to_all(
        long_chan.astype(jnp.bfloat16), "context", split_axis=1, concat_axis=0, tiled=True
    ).T
    gate = (query.astype(jnp.float32) * long_tok.astype(jnp.float32)).astype(jnp.bfloat16)
    grad_gate = lax.dot_general(
        cotangent,
        lax.all_gather(out_proj, "dp", axis=0, tiled=True),
        (((1,), (1,)), ((), ())),
        preferred_element_type=jnp.float32,
    ).astype(jnp.bfloat16)
    grad_rows = lax.psum_scatter(
        lax.dot_general(
            gate, cotangent, (((0,), (0,)), ((), ())), preferred_element_type=jnp.float32
        ),
        ("dp", "context"),
        scatter_dimension=0,
        tiled=True,
    )
    grad_query = grad_gate.astype(jnp.float32) * long_tok.astype(jnp.float32)
    grad_long = (grad_gate.astype(jnp.float32) * query.astype(jnp.float32)).astype(jnp.bfloat16)
    grad_chan = lax.all_to_all(
        grad_long.T, "context", split_axis=0, concat_axis=1, tiled=True
    ).astype(jnp.float32)
    grad_spec = forward_spectrum(grad_chan, tables)
    back_chan = (
        inverse_real(spectral_product(filter_spec, grad_spec, True), tables)
        + skip_gain[:, None] * grad_chan
    )
    filter_local = inverse_real(spectral_product(prod_spec, grad_spec, True), tables)
    grad_product = lax.all_to_all(
        back_chan.astype(jnp.bfloat16), "context", split_axis=1, concat_axis=0, tiled=True
    ).T
    scale_factor = 1.0 / math.sqrt(seq_len * lax.axis_size("dp"))
    grad_filter = (
        lax.psum_scatter(filter_local, "dp", scatter_dimension=1, tiled=True) * scale_factor
    )
    grad_skip = lax.psum(jnp.sum(grad_chan * prod_f, axis=1), "dp") * scale_factor
    grad_key = grad_product.astype(jnp.float32) * valued.astype(jnp.float32)
    grad_value = grad_product.astype(jnp.float32) * keyed.astype(jnp.float32)
    grad_mixed = jnp.concatenate([grad_query, grad_key, grad_value], 1)
    next_rows = passed_along(grad_mixed[:2].astype(jnp.bfloat16), "context", -1).astype(jnp.float32)
    grad_ext = jnp.concatenate([grad_mixed, next_rows], 0)
    grad_inputs = (
        short_taps[0] * grad_ext[:tok_rows]
        + short_taps[1] * grad_ext[1 : tok_rows + 1]
        + short_taps[2] * grad_ext[2:]
    ).astype(jnp.bfloat16)
    taps_terms = jnp.stack(
        [
            jnp.sum(grad_mixed * current, 0),
            jnp.sum(grad_mixed * once_back, 0),
            jnp.sum(grad_mixed * twice_back, 0),
        ]
    )
    grad_taps = lax.psum(taps_terms, ("dp", "context")) * scale_factor
    return (grad_inputs, grad_taps, grad_filter, grad_skip, grad_rows * scale_factor)


def solution(mesh):
    placed = (
        P(("dp", "context"), None),
        P(),
        P("context", None),
        P("context"),
        P("dp", None),
        P(("dp", "context"), None),
    )
    return jax.shard_map(
        body,
        mesh=mesh,
        in_specs=placed,
        out_specs=(
            P(("dp", "context"), None),
            P(),
            P("context", "dp"),
            P("context"),
            P(("dp", "context"), None),
        ),
        check_vma=False,
    )
```

profile of v0, /device:TPU:0, one launch (start us, length us, event | category | flops | bytes accessed | tf_op | source)
XLA Modules:
  0.0 625.5 jit_solution(3541810269681701199)
XLA Ops:
  15.6 84.6 %all-gather.2.cloned.1.call-done = bf16[2048,2048]{1,0:T(8,128)(2,1)} async-done(((bf16[512,2048]{1,0:T(8,128)(2,1)}), bf16[2048,2048]{1,0:T(8,128)(2,1)}) %all-gather.2.cloned.1.call-update) | async-done | bytes 8388624 | tf_op jit(solution)/shard_map/all_gather | solution.py:112
  100.2 6.2 fusion.21
  108.6 4.6 all-to-all-start.2
  115.5 3.9 convolution_bitcast_fusion.2
  119.5 9.1 %all-to-all-done.2 = bf16[8,256,128]{2,1,0:T(8,128)(2,1)S(1)} async-done(((bf16[8,256,128]{2,1,0:T(8,128)(2,1)}), bf16[8,256,128]{2,1,0:T(8,128)(2,1)S(1)}, u32[]{:S(2)}, u32[]{:S(2)}) %all-to-all-start.2) | async-done | bytes 524320 | tf_op jit(solution)/shard_map/all_to_all | solution.py:126
  132.6 4.2 fusion.16
  136.8 4.2 fusion.12
  143.0 2.6 pad_maximum_fusion.4
  145.5 5.5 copy.61
  151.0 4.0 fusion.68
  155.7 3.2 fusion.46
  159.0 17.8 %all_to_all.52 = bf16[256,8,128]{2,0,1:T(8,128)(2,1)S(1)} all-to-all(bf16[256,8,128]{2,0,1:T(8,128)(2,1)S(1)} %copy.52), channel_id=1, replica_groups=mesh['dp'=4,'context'=8] {'context'}, dimensions={1} | all-to-all | bytes 1048576 | tf_op jit(solution)/shard_map/all_to_all | solution.py:135
  178.2 2.8 convert_multiply_fusion.5
  181.2 17.8 %all_to_all.53 = bf16[8,256,128]{2,1,0:T(8,128)(2,1)S(1)} all-to-all(bf16[8,256,128]{2,1,0:T(8,128)(2,1)S(1)} %bitcast.96), channel_id=1, replica_groups=mesh['dp'=4,'context'=8] {'context'}, dimensions={0} | all-to-all | bytes 1048576 | tf_op jit(solution)/shard_map/all_to_all | solution.py:96
  202.0 4.1 fusion.14
  206.1 4.4 multiply_add_fusion.1
  210.5 4.6 pad_maximum_fusion.5
  215.1 5.5 copy.64
  220.6 6.1 fusion.66
  229.0 5.6 copy.58
  234.7 4.3 fusion.70
  239.0 2.8 multiply_add_fusion
  241.8 3.2 fusion.43
  245.1 17.8 %all_to_all.54 = bf16[256,8,128]{2,0,1:T(8,128)(2,1)S(1)} all-to-all(bf16[256,8,128]{2,0,1:T(8,128)(2,1)S(1)} %copy.43), channel_id=1, replica_groups=mesh['dp'=4,'context'=8] {'context'}, dimensions={1} | all-to-all | bytes 1048576 | tf_op jit(solution)/shard_map/all_to_all | solution.py:106
  263.9 2.6 copy.70
  273.5 3.0 multiply_reduce_fusion.2
  277.3 3.5 fusion.22
  282.0 9.1 %fusion.53 = f32[2048,2048]{1,0:T(8,128)} fusion(bf16[128,2048]{1,0:T(8,128)(2,1)S(1)} %copy-done, f32[2048,128]{0,1:T(8,128)S(1)} %copy-done.10, bf16[128,6144]{1,0:T(8,128)(2,1)} %copy-done.12), kind=kOutput, calls=%fused_computation.82 | convolution fusion | flops 1074528256 | bytes 18874368 | tf_op jit(solution)/shard_map/dot_general | solution.py:117
  293.5 8.9 %psum.15 = f32[256]{0:T(256)S(1)} all-reduce(f32[256]{0:T(256)S(1)} %fusion.52), channel_id=1, replica_groups=mesh['dp'=4,'context'=8] {'dp'}, use_global_device_ids=true, to_apply=%region_6.7 | all-reduce | flops 256 | bytes 2048 | tf_op jit(solution)/shard_map/psum | solution.py:142
  303.0 93.5 %all-reduce.2.cloned.1.call-done = f32[3,6144]{1,0:T(4,128)} async-done(((f32[3,6144]{1,0:T(4,128)}), f32[3,6144]{1,0:T(4,128)}) %all-reduce.2.cloned.1.call-update) | async-done | bytes 73744 | tf_op jit(solution)/shard_map/psum | solution.py:160
  398.0 29.9 %reduce-scatter.3.cloned.1.call-done = f32[256,256]{1,0:T(8,128)} async-done(((f32[256,1024]{1,0:T(8,128)}), f32[256,256]{1,0:T(8,128)}) %reduce-scatter.3.cloned.1.call-update) | async-done | bytes 262160 | tf_op jit(solution)/shard_map/reduce_scatter | solution.py:140
  429.6 187.3 %reduce-scatter.5.cloned.1.call-done = f32[64,2048]{1,0:T(8,128)} async-done(((f32[2048,2048]{1,0:T(8,128)}), f32[64,2048]{1,0:T(8,128)}) %reduce-scatter.5.cloned.1.call-update) | async-done | bytes 524304 | tf_op jit(solution)/shard_map/reduce_scatter | solution.py:116
  (100 shorter events, 44.3 us)
Async XLA Ops:
  7.2 93.1 %copy-start = (bf16[128,2048]{1,0:T(8,128)(2,1)S(1)}, bf16[128,2048]{1,0:T(8,128)(2,1)}, u32[]{:S(2)}) copy-start(bf16[128,2048]{1,0:T(8,128)(2,1)} %param.11) | copy-start | bytes 1572868
  7.2 5.3 copy-start.20
  7.2 93.0 %all-gather.2.cloned.1.call-start = ((), (), s32[]{:S(2)}) async-start(), calls=%async_computation.6 | async-start | bytes 10485760 | tf_op jit(solution)/shard_map/all_gather | solution.py:112
  8.8 3.6 collective-permute-start
  12.9 1.7 copy-start.1
  15.6 90.9 %copy-start.12 = (bf16[128,6144]{1,0:T(8,128)(2,1)}, bf16[128,6144]{1,0:T(8,128)(2,1)S(1)}, u32[]{:S(2)}) copy-start(bf16[128,6144]{1,0:T(8,128)(2,1)S(1)} %add_convert_fusion) | copy-start | bytes 4718596
  106.5 1.0 copy-start.11
  108.6 20.0 %all-to-all-start.2 = ((bf16[8,256,128]{2,1,0:T(8,128)(2,1)}), bf16[8,256,128]{2,1,0:T(8,128)(2,1)S(1)}, u32[]{:S(2)}, u32[]{:S(2)}) async-start(bf16[8,256,128]{2,1,0:T(8,128)(2,1)} %bitcast.17), calls=%async_computation.2 | async-start | bytes 1048576 | tf_op jit(solution)/shard_map/all_to_all | solution.py:126
  113.2 283.3 %all-reduce.2.cloned.1.call-start = ((), (), s32[]{:S(2)}) async-start(), calls=%async_computation.7 | async-start | bytes 196608 | tf_op jit(solution)/shard_map/psum | solution.py:160
  128.6 26.9 %copy-start.13 = (bf16[8,256,128]{2,1,0:T(8,128)(2,1)}, bf16[8,256,128]{2,1,0:T(8,128)(2,1)S(1)}, u32[]{:S(2)}) copy-start(bf16[8,256,128]{2,1,0:T(8,128)(2,1)S(1)} %all-to-all-done.2) | copy-start | bytes 1572868
  128.6 2.4 copy-start.7
  136.8 4.2 copy-start.3
  141.0 1.9 copy-start.5
  155.1 0.7 copy-start.21
  199.0 0.8 copy-start.15
  201.9 4.1 copy-start.4
  202.0 4.1 copy-start.6
  220.6 6.1 copy-start.18
  220.6 6.1 copy-start.19
  234.7 4.3 copy-start.8
  239.0 2.8 copy-start.16
  262.9 5.3 copy-start.9
  268.4 3.1 collective-permute-start.1
  271.5 1.9 copy-start.2
  277.2 150.8 %reduce-scatter.3.cloned.1.call-start = ((), (), s32[]{:S(2)}) async-start(), calls=%async_computation.8 | async-start | bytes 1310720 | tf_op jit(solution)/shard_map/reduce_scatter | solution.py:140
  277.3 4.8 copy-start.10
  282.0 334.9 %reduce-scatter.5.cloned.1.call-start = ((), (), s32[]{:S(2)}) async-start(), calls=%async_computation.9 | async-start | bytes 17301504 | tf_op jit(solution)/shard_map/reduce_scatter | solution.py:116
  291.2 1.0 copy-start.14
  291.2 1.2 copy-start.17
Sparse Core Ops, SparseCore 0:
  9.9 90.2 all-gather.1
  277.3 119.1 all-reduce.1
  399.4 28.5 reduce-scatter.2
  430.2 186.6 reduce-scatter.4
where the time goes:
time: 631 us; the launch traced here: 626 us
  waiting for transfers between devices  407 us (65%)
  blocking collectives  62.2 us (10%)
  matrix products  58.9 us (9%)
  other arithmetic  39.3 us (6%)
  local copies, waits for them, and re-layouts  35.3 us (6%)
  between operations  14.5 us (2%)
  starting transfers between devices  8.42 us (1%)
    reduce_scatter x1, waiting for transfers between devices, body(): lax.psum_scatter(lax.dot_general(gate, cotangent, (((0,), (0,)), ((), ())...  187 us
    psum x1, waiting for transfers between devices, body(): grad_taps = lax.psum(taps_terms, ('dp', 'context')) * scale_factor  93.5 us
    all_gather x1, waiting for transfers between devices, body(): lax.all_gather(out_proj, 'dp', axis=0, tiled=True)  84.6 us
    reduce_scatter x1, waiting for transfers between devices, body(): lax.psum_scatter(filter_local, 'dp', scatter_dimension=1, tiled=True)  29.9 us
    all_to_all x1, blocking collectives, body(): lax.all_to_all(back_chan.astype(jnp.bfloat16), 'context', split_axis=1, c...  17.8 us
    all_to_all x1, blocking collectives, body(): lax.all_to_all(product.T, 'context', split_axis=0, concat_axis=1, tiled=T...  17.8 us
    all_to_all x1, blocking collectives, body(): lax.all_to_all(long_chan.astype(jnp.bfloat16), 'context', split_axis=1, c...  17.8 us
    dot_general x3, matrix products, inverse_real(): undo = jnp.einsum('ckn,nm->ckm', spectrum, inner_back, precision=PRECISE)  14.4 us
  transfers between devices with their start and end apart: 7, of which 6 were waited for; matrix products, arithmetic and copies ran while one was open for 5% of the time, Pallas kernels for 0%

commit v1 on v0

--- a/solution.py
+++ b/solution.py
@@ -157,7 +157,7 @@
             jnp.sum(grad_mixed * twice_back, 0),
         ]
     )
-    grad_taps = lax.psum(taps_terms, ("dp", "context")) * scale_factor
+    grad_taps = lax.psum(lax.psum(taps_terms, "context"), "dp") * scale_factor
     return (grad_inputs, grad_taps, grad_filter, grad_skip, grad_rows * scale_factor)
 
 

time: 631 us -> 608 us (0.964)
  waiting for transfers between devices: 407 us -> 383 us
    psum x1 -> x2, waiting for transfers between devices: 93.5 us -> 70.2 us  [body(): grad_taps = lax.psum(lax.psum(taps_terms, 'context'), 'dp') * scale_factor]
  transfers between devices with their start and end apart: 7 -> 8, of which waited for: 6 -> 7; matrix products, arithmetic and copies ran while one was open for 5% -> 5% of each run, Pallas kernels for 0% -> 0%
where the time goes in v1:
time: 608 us; the launch traced here: 602 us
  waiting for transfers between devices  383 us (63%)
  blocking collectives  63.1 us (10%)
  matrix products  58.9 us (10%)
  other arithmetic  39.3 us (6%)
  local copies, waits for them, and re-layouts  35.3 us (6%)
  between operations  14.5 us (2%)
  starting transfers between devices  8.46 us (1%)
    reduce_scatter x1, waiting for transfers between devices, body(): lax.psum_scatter(lax.dot_general(gate, cotangent, (((0,), (0,)), ((), ())...  187 us
    all_gather x1, waiting for transfers between devices, body(): lax.all_gather(out_proj, 'dp', axis=0, tiled=True)  84.6 us
    psum x2, waiting for transfers between devices, body(): grad_taps = lax.psum(lax.psum(taps_terms, 'context'), 'dp') * scale_factor  70.2 us
    reduce_scatter x1, waiting for transfers between devices, body(): lax.psum_scatter(filter_local, 'dp', scatter_dimension=1, tiled=True)  28.9 us
    all_to_all x1, blocking collectives, body(): lax.all_to_all(back_chan.astype(jnp.bfloat16), 'context', split_axis=1, c...  17.8 us
    all_to_all x1, blocking collectives, body(): lax.all_to_all(product.T, 'context', split_axis=0, concat_axis=1, tiled=T...  17.8 us
    all_to_all x1, blocking collectives, body(): lax.all_to_all(long_chan.astype(jnp.bfloat16), 'context', split_axis=1, c...  17.8 us
    dot_general x3, matrix products, inverse_real(): undo = jnp.einsum('ckn,nm->ckm', spectrum, inner_back, precision=PRECISE)  14.4 us
  transfers between devices with their start and end apart: 8, of which 7 were waited for; matrix products, arithmetic and copies ran while one was open for 5% of the time, Pallas kernels for 0%

profile of v1, /device:TPU:0, one launch (start us, length us, event | category | flops | bytes accessed | tf_op | source)
XLA Modules:
  0.0 602.2 jit_solution(7970659599914391901)
XLA Ops:
  15.6 84.6 %all-gather.2.cloned.1.call-done = bf16[2048,2048]{1,0:T(8,128)(2,1)} async-done(((bf16[512,2048]{1,0:T(8,128)(2,1)}), bf16[2048,2048]{1,0:T(8,128)(2,1)}) %all-gather.2.cloned.1.call-update) | async-done | bytes 8388624 | tf_op jit(solution)/shard_map/all_gather | solution.py:112
  100.2 6.2 %fusion.21 = f32[128,2048]{1,0:T(8,128)S(1)} fusion(bf16[128,2048]{1,0:T(8,128)(2,1)S(1)} %copy-done, bf16[2048,2048]{1,0:T(8,128)(2,1)} %all-gather.2.cloned.1.call-done), kind=kOutput, calls=%fused_computation.36 | convolution fusion | flops 1074266112 | bytes 9961472 | tf_op jit(solution)/shard_map/dot_general | solution.py:110
  108.6 4.6 all-to-all-start.2
  115.5 3.9 convolution_bitcast_fusion.2
  119.5 9.1 %all-to-all-done.2 = bf16[8,256,128]{2,1,0:T(8,128)(2,1)S(1)} async-done(((bf16[8,256,128]{2,1,0:T(8,128)(2,1)}), bf16[8,256,128]{2,1,0:T(8,128)(2,1)S(1)}, u32[]{:S(2)}, u32[]{:S(2)}) %all-to-all-start.2) | async-done | bytes 524320 | tf_op jit(solution)/shard_map/all_to_all | solution.py:126
  132.6 4.2 fusion.16
  136.8 4.2 fusion.12
  143.0 2.6 pad_maximum_fusion.4
  145.5 5.5 copy.61
  151.0 4.0 fusion.68
  155.7 3.2 fusion.46
  159.0 17.8 %all_to_all.52 = bf16[256,8,128]{2,0,1:T(8,128)(2,1)S(1)} all-to-all(bf16[256,8,128]{2,0,1:T(8,128)(2,1)S(1)} %copy.52), channel_id=1, replica_groups=mesh['dp'=4,'context'=8] {'context'}, dimensions={1} | all-to-all | bytes 1048576 | tf_op jit(solution)/shard_map/all_to_all | solution.py:135
  178.2 2.8 convert_multiply_fusion.5
  181.2 17.8 %all_to_all.53 = bf16[8,256,128]{2,1,0:T(8,128)(2,1)S(1)} all-to-all(bf16[8,256,128]{2,1,0:T(8,128)(2,1)S(1)} %bitcast.96), channel_id=1, replica_groups=mesh['dp'=4,'context'=8] {'context'}, dimensions={0} | all-to-all | bytes 1048576 | tf_op jit(solution)/shard_map/all_to_all | solution.py:96
  202.0 4.1 fusion.14
  206.1 4.4 multiply_add_fusion.1
  210.5 4.6 pad_maximum_fusion.5
  215.1 5.5 copy.64
  220.6 6.1 %fusion.66 = f32[256,16,256]{2,1,0:T(8,128)} fusion(f32[256,16,256]{2,1,0:T(8,128)} %copy.64, f32[128,128]{0,1:T(8,128)S(1)} %get-tuple-element.42, f32[128,128]{0,1:T(8,128)S(1)} %get-tuple-element.41, f32[128,128]{0,1:T(8,128)S(1)} %fusion.83), kind=kOutput, calls=%fused_computation.99 | convolution fusion | flops 1610809344 | bytes 8585216 | tf_op jit(solution)/shard_map/ckn,nm->ckm/dot_general | solution.py:73
  229.0 5.6 copy.58
  234.7 4.3 fusion.70
  239.0 2.8 multiply_add_fusion
  241.8 3.2 fusion.43
  245.1 17.8 %all_to_all.54 = bf16[256,8,128]{2,0,1:T(8,128)(2,1)S(1)} all-to-all(bf16[256,8,128]{2,0,1:T(8,128)(2,1)S(1)} %copy.43), channel_id=1, replica_groups=mesh['dp'=4,'context'=8] {'context'}, dimensions={1} | all-to-all | bytes 1048576 | tf_op jit(solution)/shard_map/all_to_all | solution.py:106
  273.5 3.0 multiply_reduce_fusion.2
  277.3 50.4 %all-reduce.3.cloned.1.call-done = f32[3,6144]{1,0:T(4,128)} async-done(((f32[3,6144]{1,0:T(4,128)}), f32[3,6144]{1,0:T(4,128)}) %all-reduce.3.cloned.1.call-update) | async-done | bytes 73744 | tf_op jit(solution)/shard_map/psum | solution.py:160
  327.7 3.5 fusion.22
  332.5 9.1 %fusion.53 = f32[2048,2048]{1,0:T(8,128)} fusion(bf16[128,2048]{1,0:T(8,128)(2,1)S(1)} %copy-done, f32[2048,128]{0,1:T(8,128)S(1)} %copy-done.10, bf16[128,6144]{1,0:T(8,128)(2,1)} %copy-done.12), kind=kOutput, calls=%fused_computation.82 | convolution fusion | flops 1074528256 | bytes 18874368 | tf_op jit(solution)/shard_map/dot_general | solution.py:117
  343.9 9.8 %psum.23 = f32[256]{0:T(256)S(1)} all-reduce(f32[256]{0:T(256)S(1)} %fusion.52), channel_id=1, replica_groups=mesh['dp'=4,'context'=8] {'dp'}, use_global_device_ids=true, to_apply=%region_7.8 | all-reduce | flops 256 | bytes 2048 | tf_op jit(solution)/shard_map/psum | solution.py:142
  354.3 19.8 %all-reduce.5.cloned.1.call-done = f32[3,6144]{1,0:T(4,128)} async-done(((f32[3,6144]{1,0:T(4,128)}), f32[3,6144]{1,0:T(4,128)}) %all-reduce.5.cloned.1.call-update) | async-done | bytes 73744 | tf_op jit(solution)/shard_map/psum | solution.py:160
  375.7 28.9 %reduce-scatter.3.cloned.1.call-done = f32[256,256]{1,0:T(8,128)} async-done(((f32[256,1024]{1,0:T(8,128)}), f32[256,256]{1,0:T(8,128)}) %reduce-scatter.3.cloned.1.call-update) | async-done | bytes 262160 | tf_op jit(solution)/shard_map/reduce_scatter | solution.py:140
  406.3 187.2 %reduce-scatter.5.cloned.1.call-done = f32[64,2048]{1,0:T(8,128)} async-done(((f32[2048,2048]{1,0:T(8,128)}), f32[64,2048]{1,0:T(8,128)}) %reduce-scatter.5.cloned.1.call-update) | async-done | bytes 524304 | tf_op jit(solution)/shard_map/reduce_scatter | solution.py:116
  (103 shorter events, 46.9 us)
Async XLA Ops:
  7.2 93.1 %copy-start = (bf16[128,2048]{1,0:T(8,128)(2,1)S(1)}, bf16[128,2048]{1,0:T(8,128)(2,1)}, u32[]{:S(2)}) copy-start(bf16[128,2048]{1,0:T(8,128)(2,1)} %param.11) | copy-start | bytes 1572868
  7.2 5.3 copy-start.20
  7.2 93.0 %all-gather.2.cloned.1.call-start = ((), (), s32[]{:S(2)}) async-start(), calls=%async_computation.6 | async-start | bytes 10485760 | tf_op jit(solution)/shard_map/all_gather | solution.py:112
  8.8 3.6 collective-permute-start
  12.9 1.7 copy-start.1
  15.6 90.9 %copy-start.12 = (bf16[128,6144]{1,0:T(8,128)(2,1)}, bf16[128,6144]{1,0:T(8,128)(2,1)S(1)}, u32[]{:S(2)}) copy-start(bf16[128,6144]{1,0:T(8,128)(2,1)S(1)} %add_convert_fusion) | copy-start | bytes 4718596
  106.5 1.0 copy-start.11
  108.6 20.0 %all-to-all-start.2 = ((bf16[8,256,128]{2,1,0:T(8,128)(2,1)}), bf16[8,256,128]{2,1,0:T(8,128)(2,1)S(1)}, u32[]{:S(2)}, u32[]{:S(2)}) async-start(bf16[8,256,128]{2,1,0:T(8,128)(2,1)} %bitcast.17), calls=%async_computation.2 | async-start | bytes 1048576 | tf_op jit(solution)/shard_map/all_to_all | solution.py:126
  113.2 214.4 %all-reduce.3.cloned.1.call-start = ((), (), s32[]{:S(2)}) async-start(), calls=%async_computation.7 | async-start | bytes 196608 | tf_op jit(solution)/shard_map/psum | solution.py:160
  128.6 26.9 %copy-start.13 = (bf16[8,256,128]{2,1,0:T(8,128)(2,1)}, bf16[8,256,128]{2,1,0:T(8,128)(2,1)S(1)}, u32[]{:S(2)}) copy-start(bf16[8,256,128]{2,1,0:T(8,128)(2,1)S(1)} %all-to-all-done.2) | copy-start | bytes 1572868
  128.6 2.4 copy-start.7
  136.8 4.2 copy-start.3
  141.0 1.9 copy-start.5
  155.1 0.7 copy-start.21
  199.0 0.8 copy-start.15
  201.9 4.1 copy-start.4
  202.0 4.1 copy-start.6
  220.6 6.1 %copy-start.18 = (f32[256,16,128]{0,2,1:T(8,128)S(1)}, f32[256,16,128]{0,2,1:T(8,128)}, u32[]{:S(2)}) copy-start(f32[256,16,128]{0,2,1:T(8,128)} %get-tuple-element.26) | copy-start | bytes 6291460
  220.6 6.1 %copy-start.19 = (f32[256,16,128]{0,2,1:T(8,128)S(1)}, f32[256,16,128]{0,2,1:T(8,128)}, u32[]{:S(2)}) copy-start(f32[256,16,128]{0,2,1:T(8,128)} %get-tuple-element.27) | copy-start | bytes 6291460
  234.7 4.3 copy-start.8
  239.0 2.8 copy-start.16
  262.9 5.3 copy-start.9
  268.4 3.1 collective-permute-start.1
  271.5 1.9 copy-start.2
  277.2 96.9 %all-reduce.5.cloned.1.call-start = ((), (), s32[]{:S(2)}) async-start(), calls=%async_computation.8 | async-start | bytes 196608 | tf_op jit(solution)/shard_map/psum | solution.py:160
  327.7 77.0 %reduce-scatter.3.cloned.1.call-start = ((), (), s32[]{:S(2)}) async-start(), calls=%async_computation.9 | async-start | bytes 1310720 | tf_op jit(solution)/shard_map/reduce_scatter | solution.py:140
  327.7 4.8 copy-start.10
  332.4 261.2 %reduce-scatter.5.cloned.1.call-start = ((), (), s32[]{:S(2)}) async-start(), calls=%async_computation.10 | async-start | bytes 17301504 | tf_op jit(solution)/shard_map/reduce_scatter | solution.py:116
  341.6 1.0 copy-start.14
  341.6 1.2 copy-start.17
Sparse Core Ops, SparseCore 0:
  9.9 90.2 all-gather.1
  277.3 50.2 all-reduce.2
  330.8 43.3 all-reduce.4
  376.9 27.7 reduce-scatter.2
  406.9 186.6 reduce-scatter.4
